TPU v7x, 512 devices: a whole 4x4x16 slice. The times are simulated.
512 devices in a mesh: mol: 128 (over z, y, core), traj: 4 (over x).
Axes of the slice: x: 4, y: 4, z: 16, core: 2. Of those that a mesh axis runs over, the one named last changes fastest.
Arguments:
- positions: float32 [64, 16384], P('traj', 'mol'), parts along dimension 0, may hold values from -1.2 to 1.2
- velocities: float32 [64, 16384], P('traj', 'mol'), parts along dimension 0, may hold values from -3 to 3
- amplitudes: float32 [4096, 64], P('mol', 'traj'), parts along dimension 1, may hold values from -6 to 6
- momenta: float32 [4096, 64], P('mol', 'traj'), parts along dimension 1, may hold values from -6 to 6
- sites: int32 [16384], P('mol'), may hold values from 0 to 32767
- wavevectors: int32 [4096], replicated, may hold values from 1 to 32767
- mode_freq: float32 [4096], P('mol'), may hold values from 0.5 to 2
- coupling: float32 [4096], P('mol'), may hold values from 0.0078125 to 0.03125
- depth: float32 [16384], P('mol'), may hold values from 0.5 to 2
- stiffness: float32 [16384], P('mol'), may hold values from 0.8 to 1.5
- dipole_slope: float32 [16384], P('mol'), may hold values from -4 to 4
Outputs:
- final_positions: float32 [64, 16384], P('traj', 'mol'), parts along dimension 0
- final_velocities: float32 [64, 16384], P('traj', 'mol'), parts along dimension 0
- final_amplitudes: float32 [4096, 64], P('mol', 'traj'), parts along dimension 1
- final_momenta: float32 [4096, 64], P('mol', 'traj'), parts along dimension 1
There are 4 independent parts, one for each index of `traj`. A program takes and returns all parts, laid end to end along the dimension named above; an argument that names none is the same for every part. Nothing has to cross between parts.
All inputs are finite; a program needn't handle non-finite values.
Results may differ from a plain program's by a relative error of at most 0.0003.
Values sent between devices are 32-bit elements; how exact they have to be, the bound alone decides.
No kernel may reach another device: no remote copies, remote signals or barrier semaphores. Data moves between devices by JAX's collectives and lax.ppermute only.
A program may use at most 64 MiB of HBM per device.

v0:
```python
import math
import jax
import jax.numpy as jnp
from jax import lax
from jax.sharding import PartitionSpec as P

STEPS = 2


def phase_tile(waves, sites, lattice):
    high = sites // 256
    low = sites % 256
    first = waves[:, None] * high[None, :] % lattice
    residue = (first * 256 + waves[:, None] * low[None, :]) % lattice
    angle = residue.astype(jnp.float32) * (2.0 * math.pi / lattice)
    return jnp.sin(angle)


def project_dipole(tile, dipole):
    return lax.dot_general(
        tile,
        dipole,
        (((1,), (1,)), ((), ())),
        precision=lax.Precision.HIGHEST,
        preferred_element_type=jnp.float32,
    )


def project_modes(weighted, tile):
    return lax.dot_general(
        weighted,
        tile,
        (((0,), (0,)), ((), ())),
        precision=lax.Precision.HIGHEST,
        preferred_element_type=jnp.float32,
    )


def advance_bonds(positions, velocities, pull, depth, stiffness, dipole_slope, step_time):
    damped = jnp.exp(-stiffness[None, :] * positions)
    force = (
        -2.0 * depth[None, :] * stiffness[None, :] * (1.0 - damped) * damped
        - dipole_slope[None, :] * pull
    )
    velocities = velocities + step_time * force
    positions = positions + step_time * velocities
    return (positions, velocities)


def local(
    positions,
    velocities,
    amplitudes,
    momenta,
    sites,
    wavevectors,
    mode_freq,
    coupling,
    depth,
    stiffness,
    dipole_slope,
):
    step_time = 0.2
    lattice = 2 * sites.shape[0] * lax.axis_size("mol")
    owned_rows = amplitudes.shape[0]
    stored = phase_tile(wavevectors, sites, lattice)

    def tile_rows():
        return stored

    for step in range(STEPS):
        dipole = dipole_slope[None, :] * positions

        def drive_term(start, count, dipole=dipole):
            return project_dipole(tile_rows(), dipole)

        drive = lax.psum_scatter(
            drive_term(jnp.int32(0), lax.axis_size("mol") * owned_rows),
            "mol",
            scatter_dimension=0,
            tiled=True,
        )
        momenta = momenta + step_time * (
            -(mode_freq * mode_freq)[:, None] * amplitudes - coupling[:, None] * drive
        )
        amplitudes = amplitudes + step_time * momenta
        weighted = coupling[:, None] * amplitudes
        pull = project_modes(lax.all_gather(weighted, "mol", axis=0, tiled=True), tile_rows())
        positions, velocities = advance_bonds(
            positions, velocities, pull, depth, stiffness, dipole_slope, step_time
        )
    return (positions, velocities, amplitudes, momenta)


def solution(mesh):
    return jax.shard_map(
        local,
        mesh=mesh,
        in_specs=(
            P("traj", "mol"),
            P("traj", "mol"),
            P("mol", "traj"),
            P("mol", "traj"),
            P("mol"),
            P(),
            P("mol"),
            P("mol"),
            P("mol"),
            P("mol"),
            P("mol"),
        ),
        out_specs=(P("traj", "mol"), P("traj", "mol"), P("mol", "traj"), P("mol", "traj")),
        check_vma=False,
    )
```

profile of v0, /device:TPU:1, one launch (start us, length us, event | category | flops | bytes accessed | tf_op | source)
XLA Modules:
  0.0 796.6 jit_solution(9365872709216338628)
XLA Ops:
  7.2 0.0 reduce-scatter.7.cloned.1.call-start
  7.2 0.7 and_select_fusion.1
  7.9 13.8 %fusion.17 = f32[4096,16]{1,0:T(8,128)} fusion(s32[128]{0:T(128)S(1)} %get-tuple-element.10, s32[128]{0:T(128)S(1)} %get-tuple-element.9, s32[4096]{0:T(1024)} %param.16, f32[16,128]{1,0:T(8,128)} %param.11, f32[128]{0:T(128)} %param.21), kind=kOutput, calls=%fused_computation.24 | convolution fusion | flops 115345408 | bytes 288256
  21.7 0.0 copy-start
  21.7 0.0 copy-start.1
  21.7 0.0 copy-start.2
  21.7 0.0 reduce-scatter.7.cloned.1.call-update
  21.7 0.0 reduce-scatter.9.cloned.1.call-start
  21.8 0.5 copy-done.8
  22.3 0.0 copy-done.3
  22.3 0.0 copy-done.4
  22.3 257.0 %reduce-scatter.7.cloned.1.call-done = f32[32,16]{1,0:T(8,128)} async-done(((f32[4096,16]{1,0:T(8,128)}), f32[32,16]{1,0:T(8,128)}) %reduce-scatter.7.cloned.1.call-update) | async-done | bytes 2064
  279.3 0.8 copy.20
  280.1 0.0 copy-done
  280.1 0.0 copy-done.1
  280.1 0.0 copy-start.5
  280.2 0.0 copy-start.6
  280.2 0.0 copy-start.7
  280.2 0.0 copy-start.9
  280.2 111.7 %all-gather = f32[128,32,16]{1,2,0:T(8,128)S(1)} all-gather(f32[1,32,16]{1,2,0:T(8,128)S(1)} %multiply_bitcast_fusion.1), channel_id=1, replica_groups=mesh['mol'=128,'traj'=4] {'mol'}, dimensions={0}, use_global_device_ids=true | all-gather | bytes 264192 | tf_op jit(solution)/shard_map/all_gather | solution.py:88
  391.9 0.3 copy.17
  392.2 0.5 reshape.21
  392.8 10.0 %fusion.12 = f32[16,128]{1,0:T(8,128)S(1)} fusion(f32[16,128]{1,0:T(8,128)S(1)} %copy-done.6, f32[4096,16]{0,1:T(8,128)S(1)} %reshape.21, s32[128]{0:T(128)S(1)} %get-tuple-element.10, s32[128]{0:T(128)S(1)} %get-tuple-element.9, s32[4096]{0:T(1024)S(1)} %copy-done.5, f32[16,128]{1,0:T(8,128)S(1)} %copy-done.7, f32[128]{0:T(128)S(1)} %copy-done.9, ...), kind=kOutput, calls=%fused_computation.22 | convolution fusion | flops 115359744 | bytes 305664 | tf_op jit(solution)/shard_map/dot_general | solution.py:30
  402.8 13.3 %fusion.14 = f32[4096,16]{1,0:T(8,128)} fusion(s32[128]{0:T(128)S(1)} %get-tuple-element.10, s32[128]{0:T(128)S(1)} %get-tuple-element.9, s32[4096]{0:T(1024)S(1)} %copy-done.5, f32[128]{0:T(128)S(1)} %copy-done.9, f32[16,128]{1,0:T(8,128)S(1)} %copy-done.7, f32[16,128]{1,0:T(8,128)S(1)} %fusion.12), kind=kOutput, calls=%fused_computation.23 | convolution fusion | flops 115349504 | bytes 296448
  416.1 0.0 reduce-scatter.9.cloned.1.call-update
  416.1 249.2 %reduce-scatter.9.cloned.1.call-done = f32[32,16]{1,0:T(8,128)} async-done(((f32[4096,16]{1,0:T(8,128)}), f32[32,16]{1,0:T(8,128)}) %reduce-scatter.9.cloned.1.call-update) | async-done | bytes 2064
  665.3 0.8 copy.22
  666.1 0.6 multiply_bitcast_fusion
  666.7 111.6 %all-gather.1 = f32[128,32,16]{1,2,0:T(8,128)S(1)} all-gather(f32[1,32,16]{1,2,0:T(8,128)S(1)} %get-tuple-element.4), channel_id=1, replica_groups=mesh['mol'=128,'traj'=4] {'mol'}, dimensions={0}, use_global_device_ids=true | all-gather | bytes 264192 | tf_op jit(solution)/shard_map/all_gather | solution.py:88
  778.2 0.3 copy.18
  778.6 0.5 reshape.23
  779.1 10.7 %multiply_add_fusion = (f32[16,128]{1,0:T(8,128)}, f32[16,128]{1,0:T(8,128)}) fusion(f32[16,128]{1,0:T(8,128)S(1)} %copy-done.7, f32[16,128]{1,0:T(8,128)S(1)} %fusion.12, f32[4096,16]{0,1:T(8,128)S(1)} %reshape.23, s32[128]{0:T(128)S(1)} %get-tuple-element.10, s32[128]{0:T(128)S(1)} %get-tuple-element.9, s32[4096]{0:T(1024)S(1)} %copy-done.5, ...), kind=kOutput, calls=%fused_computation.25 | convolution fusion | flops 115367936 | bytes 313856 | tf_op jit(solution)/shard_map/dot_general | solution.py:30
  (11 shorter events, 0.0 us)
Async XLA Ops:
  7.2 272.2 %reduce-scatter.7.cloned.1.call-start = ((), (), s32[]{:S(2)}) async-start(), calls=%async_computation.2 | async-start | bytes 2113536
  21.7 0.7 copy-start.8
  21.7 0.7 copy-start.3
  21.7 0.7 copy-start.4
  21.7 258.5 %copy-start = (f32[32,16]{0,1:T(8,128)S(1)}, f32[32,16]{0,1:T(8,128)}, u32[]{:S(2)}) copy-start(f32[32,16]{0,1:T(8,128)} %param.13) | copy-start | bytes 6148
  21.7 258.4 %copy-start.1 = (f32[32,16]{0,1:T(8,128)S(1)}, f32[32,16]{0,1:T(8,128)}, u32[]{:S(2)}) copy-start(f32[32,16]{0,1:T(8,128)} %param.14) | copy-start | bytes 6148
  21.7 258.4 %copy-start.2 = (f32[32]{0:T(128)S(1)}, f32[32]{0:T(128)}, u32[]{:S(2)}) copy-start(f32[32]{0:T(128)} %param.18) | copy-start | bytes 388
  21.7 643.5 %reduce-scatter.9.cloned.1.call-start = ((), (), s32[]{:S(2)}) async-start(), calls=%async_computation.3 | async-start | bytes 2113536
  280.1 112.6 %copy-start.5 = (s32[4096]{0:T(1024)S(1)}, s32[4096]{0:T(1024)}, u32[]{:S(2)}) copy-start(s32[4096]{0:T(1024)} %param.16) | copy-start | bytes 49156
  280.2 112.6 %copy-start.6 = (f32[16,128]{1,0:T(8,128)S(1)}, f32[16,128]{1,0:T(8,128)}, u32[]{:S(2)}) copy-start(f32[16,128]{1,0:T(8,128)} %param.12) | copy-start | bytes 24580
  280.2 112.6 %copy-start.7 = (f32[16,128]{1,0:T(8,128)S(1)}, f32[16,128]{1,0:T(8,128)}, u32[]{:S(2)}) copy-start(f32[16,128]{1,0:T(8,128)} %param.11) | copy-start | bytes 24580
  280.2 112.6 %copy-start.9 = (f32[128]{0:T(128)S(1)}, f32[128]{0:T(128)}, u32[]{:S(2)}) copy-start(f32[128]{0:T(128)} %param.21) | copy-start | bytes 1540
Sparse Core Ops, SparseCore 0:
  21.8 257.4 reduce-scatter.6
  416.2 248.9 reduce-scatter.8
where the time goes:
time: 797 us
  waiting for transfers between devices  506 us (63%)
  blocking collectives  223 us (28%)
  matrix products  47.8 us (6%)
  between operations  14.2 us (2%)
    unnamed x4, waiting for transfers between devices  506 us
    all_gather x2, blocking collectives, local(): lax.all_gather(weighted, 'mol', axis=0, tiled=True)  223 us
    unnamed x2, matrix products  27 us
    dot_general x2, matrix products, project_modes(): lax.dot_general(weighted, tile, (((0,), (0,)), ((), ())), precision=lax.P...  20.8 us
  transfers between devices with their start and end apart: 2, of which 2 were waited for; matrix products, arithmetic and copies ran while one was open for 0% of the time, Pallas kernels for 0%

commit v1 on v0

--- a/solution.py
+++ b/solution.py
@@ -85,7 +85,12 @@
         )
         amplitudes = amplitudes + step_time * momenta
         weighted = coupling[:, None] * amplitudes
-        pull = project_modes(lax.all_gather(weighted, "mol", axis=0, tiled=True), tile_rows())
+        pull = project_modes(
+            jnp.concatenate(
+                lax.all_to_all(jnp.stack([weighted] * lax.axis_size("mol")), "mol", 0, 0), axis=0
+            ),
+            tile_rows(),
+        )
         positions, velocities = advance_bonds(
             positions, velocities, pull, depth, stiffness, dipole_slope, step_time
         )

time: 797 us -> 665 us (0.83)
  blocking collectives: 223 us -> 44.3 us
  starting transfers between devices: 0.08 us -> 24.2 us
  waiting for transfers between devices: 506 us -> 522 us
    all_gather x2 -> x0, blocking collectives: 223 us -> none  [local(): lax.all_gather(weighted, 'mol', axis=0, tiled=True)]
    all_to_all x0 -> x1, blocking collectives: none -> 44.3 us  [local(): lax.all_to_all(jnp.stack([weighted] * lax.axis_size('mol')), 'mol', 0, 0)]
    all_to_all x0 -> x1, starting transfers between devices: none -> 23.9 us  [local(): lax.all_to_all(jnp.stack([weighted] * lax.axis_size('mol')), 'mol', 0, 0)]
    all_to_all x0 -> x1, waiting for transfers between devices: none -> 20.2 us  [local(): lax.all_to_all(jnp.stack([weighted] * lax.axis_size('mol')), 'mol', 0, 0)]
  transfers between devices with their start and end apart: 2 -> 3, of which waited for: 2 -> 3; matrix products, arithmetic and copies ran while one was open for 0% -> 0% of each run, Pallas kernels for 0% -> 0%
where the time goes in v1:
time: 665 us; the launch traced here: 663 us
  waiting for transfers between devices  522 us (78%)
  matrix products  47.6 us (7%)
  blocking collectives  44.3 us (7%)
  starting transfers between devices  24.2 us (4%)
  between operations  14.2 us (2%)
  local copies, waits for them, and re-layouts  6.68 us (1%)
    unnamed x4, waiting for transfers between devices  502 us
    all_to_all x1, blocking collectives, local(): lax.all_to_all(jnp.stack([weighted] * lax.axis_size('mol')), 'mol', 0, 0)  44.3 us
    unnamed x2, matrix products  27 us
    all_to_all x1, starting transfers between devices, local(): lax.all_to_all(jnp.stack([weighted] * lax.axis_size('mol')), 'mol', 0, 0)  23.9 us
    dot_general x2, matrix products, project_modes(): lax.dot_general(weighted, tile, (((0,), (0,)), ((), ())), precision=lax.P...  20.6 us
    all_to_all x1, waiting for transfers between devices, local(): lax.all_to_all(jnp.stack([weighted] * lax.axis_size('mol')), 'mol', 0, 0)  20.2 us
  transfers between devices with their start and end apart: 3, of which 3 were waited for; matrix products, arithmetic and copies ran while one was open for 0% of the time, Pallas kernels for 0%

profile of v1, /device:TPU:1, one launch (start us, length us, event | category | flops | bytes accessed | tf_op | source)
XLA Modules:
  0.0 663.3 jit_solution(4919036158424393569)
XLA Ops:
  7.2 0.0 reduce-scatter.7.cloned.1.call-start
  7.2 0.7 and_select_fusion.1
  7.9 13.8 %fusion.17 = f32[4096,16]{1,0:T(8,128)} fusion(s32[128]{0:T(128)S(1)} %get-tuple-element.10, s32[128]{0:T(128)S(1)} %get-tuple-element.9, s32[4096]{0:T(1024)} %param.16, f32[16,128]{1,0:T(8,128)} %param.11, f32[128]{0:T(128)} %param.21), kind=kOutput, calls=%fused_computation.24 | convolution fusion | flops 115345408 | bytes 288256
  21.7 0.0 copy-start.3
  21.7 0.0 reduce-scatter.7.cloned.1.call-update
  21.7 0.6 copy-done.8
  22.3 257.0 %reduce-scatter.7.cloned.1.call-done = f32[32,16]{1,0:T(8,128)} async-done(((f32[4096,16]{1,0:T(8,128)}), f32[32,16]{1,0:T(8,128)}) %reduce-scatter.7.cloned.1.call-update) | async-done | bytes 2064
  279.3 0.8 copy.20
  280.1 0.1 broadcast_bitcast_fusion.1
  280.2 1.2 reshape.36
  281.4 23.9 %all-to-all-start = ((f32[128,1,512]{2,1,0:T(1,128)}), f32[128,1,512]{2,1,0:T(1,128)S(1)}, u32[]{:S(2)}, u32[]{:S(2)}) async-start(f32[128,1,512]{2,1,0:T(1,128)} %reshape.36), calls=%async_computation | async-start | bytes 524288 | tf_op jit(solution)/shard_map/all_to_all | solution.py:90
  305.3 0.2 reduce-scatter.9.cloned.1.call-start
  305.6 20.2 %all-to-all-done = f32[128,1,512]{2,1,0:T(1,128)S(1)} async-done(((f32[128,1,512]{2,1,0:T(1,128)}), f32[128,1,512]{2,1,0:T(1,128)S(1)}, u32[]{:S(2)}, u32[]{:S(2)}) %all-to-all-start) | async-done | bytes 262176 | tf_op jit(solution)/shard_map/all_to_all | solution.py:90
  325.7 0.5 broadcast.102
  326.2 1.3 reduce
  327.6 0.3 reshape.37
  327.8 0.3 copy.17
  328.2 0.5 reshape.30
  328.7 10.1 %fusion.12 = f32[16,128]{1,0:T(8,128)S(1)} fusion(f32[16,128]{1,0:T(8,128)S(1)} %copy-done.6, f32[4096,16]{0,1:T(8,128)S(1)} %reshape.30, s32[128]{0:T(128)S(1)} %get-tuple-element.10, s32[128]{0:T(128)S(1)} %get-tuple-element.9, s32[4096]{0:T(1024)S(1)} %copy-done.5, f32[16,128]{1,0:T(8,128)S(1)} %copy-done.7, f32[128]{0:T(128)S(1)} %copy-done.9, ...), kind=kOutput, calls=%fused_computation.22 | convolution fusion | flops 115359744 | bytes 305664 | tf_op jit(solution)/shard_map/dot_general | solution.py:30
  338.8 13.3 %fusion.14 = f32[4096,16]{1,0:T(8,128)} fusion(s32[128]{0:T(128)S(1)} %get-tuple-element.10, s32[128]{0:T(128)S(1)} %get-tuple-element.9, s32[4096]{0:T(1024)S(1)} %copy-done.5, f32[128]{0:T(128)S(1)} %copy-done.9, f32[16,128]{1,0:T(8,128)S(1)} %copy-done.7, f32[16,128]{1,0:T(8,128)S(1)} %fusion.12), kind=kOutput, calls=%fused_computation.23 | convolution fusion | flops 115349504 | bytes 296448
  352.1 0.0 reduce-scatter.9.cloned.1.call-update
  352.1 245.2 %reduce-scatter.9.cloned.1.call-done = f32[32,16]{1,0:T(8,128)} async-done(((f32[4096,16]{1,0:T(8,128)}), f32[32,16]{1,0:T(8,128)}) %reduce-scatter.9.cloned.1.call-update) | async-done | bytes 2064
  597.3 0.8 copy.22
  598.1 0.6 broadcast_multiply_fusion
  598.7 0.1 broadcast_bitcast_fusion
  598.8 0.5 reshape.38
  599.2 44.3 %all_to_all.10 = f32[128,1,512]{2,1,0:T(1,128)S(1)} all-to-all(f32[128,1,512]{2,1,0:T(1,128)S(1)} %reshape.38), channel_id=1, replica_groups=mesh['mol'=128,'traj'=4] {'mol'}, dimensions={0} | all-to-all | bytes 524288 | tf_op jit(solution)/shard_map/all_to_all | solution.py:90
  643.6 1.3 reduce.1
  644.8 0.3 reshape.39
  645.1 0.3 copy.18
  645.5 0.5 reshape.31
  645.9 10.5 %multiply_add_fusion = (f32[16,128]{1,0:T(8,128)}, f32[16,128]{1,0:T(8,128)}) fusion(f32[16,128]{1,0:T(8,128)S(1)} %copy-done.7, f32[16,128]{1,0:T(8,128)S(1)} %fusion.12, f32[4096,16]{0,1:T(8,128)S(1)} %reshape.31, s32[128]{0:T(128)S(1)} %get-tuple-element.10, s32[128]{0:T(128)S(1)} %get-tuple-element.9, s32[4096]{0:T(1024)S(1)} %copy-done.5, ...), kind=kOutput, calls=%fused_computation.25 | convolution fusion | flops 115367936 | bytes 313856 | tf_op jit(solution)/shard_map/dot_general | solution.py:30
  (21 shorter events, 0.1 us)
Async XLA Ops:
  7.2 272.2 %reduce-scatter.7.cloned.1.call-start = ((), (), s32[]{:S(2)}) async-start(), calls=%async_computation.4 | async-start | bytes 2113536
  21.7 0.7 copy-start.8
  21.7 258.5 %copy-start = (f32[32,16]{0,1:T(8,128)S(1)}, f32[32,16]{0,1:T(8,128)}, u32[]{:S(2)}) copy-start(f32[32,16]{0,1:T(8,128)} %param.13) | copy-start | bytes 6148
  21.7 258.5 %copy-start.1 = (f32[32,16]{0,1:T(8,128)S(1)}, f32[32,16]{0,1:T(8,128)}, u32[]{:S(2)}) copy-start(f32[32,16]{0,1:T(8,128)} %param.14) | copy-start | bytes 6148
  21.7 258.5 %copy-start.2 = (f32[32]{0:T(128)S(1)}, f32[32]{0:T(128)}, u32[]{:S(2)}) copy-start(f32[32]{0:T(128)} %param.18) | copy-start | bytes 388
  21.7 283.8 %copy-start.3 = (f32[128]{0:T(128)S(1)}, f32[128]{0:T(128)}, u32[]{:S(2)}) copy-start(f32[128]{0:T(128)} %param.20) | copy-start | bytes 1540
  21.7 283.8 %copy-start.4 = (f32[128]{0:T(128)S(1)}, f32[128]{0:T(128)}, u32[]{:S(2)}) copy-start(f32[128]{0:T(128)} %param.19) | copy-start | bytes 1540
  281.4 44.3 %all-to-all-start = ((f32[128,1,512]{2,1,0:T(1,128)}), f32[128,1,512]{2,1,0:T(1,128)S(1)}, u32[]{:S(2)}, u32[]{:S(2)}) async-start(f32[128,1,512]{2,1,0:T(1,128)} %reshape.36), calls=%async_computation | async-start | bytes 524288 | tf_op jit(solution)/shard_map/all_to_all | solution.py:90
  305.3 292.0 %reduce-scatter.9.cloned.1.call-start = ((), (), s32[]{:S(2)}) async-start(), calls=%async_computation.5 | async-start | bytes 2113536
  327.5 1.2 copy-start.5
  327.5 1.2 copy-start.6
  327.5 1.2 copy-start.7
  327.5 1.2 copy-start.9
Sparse Core Ops, SparseCore 0:
  21.8 257.4 reduce-scatter.6
  352.2 245.0 reduce-scatter.8
